TPU v7x, 32 devices: a whole 2x2x4 slice. The times are simulated.
32 devices in a mesh: sky: 4 (over y, x), visit: 4 (over z), patch: 2 (over core).
Axes of the slice: x: 2, y: 2, z: 4, core: 2. Of those that a mesh axis runs over, the one named last changes fastest.
Arguments:
- template_store: float32 [4, 128, 2048], P('visit', 'patch', 'sky'), may hold values from -6 to 6
- science: float32 [4, 128, 2048], P('visit', 'patch', 'sky'), may hold values from -40 to 40
- owner_visit: int32 [4, 2], P('sky', 'patch'), may hold values from 0 to 3, as said below
- stamp_offset: int32 [2, 4, 2, 32], P(None, 'visit', 'patch', 'sky'), may hold values from 0 to 32
Outputs:
- difference: float32 [4, 128, 2048], P('visit', 'patch', 'sky')
Inputs may be any that keep to these rules, and one draw needn't show every extreme that they name: owner_visit[s, p] = (owner_visit[s, 0] + p) mod 4; only that visit's slot of template_store holds the current coadd of sky tile s, patch p.
All inputs are finite; a program needn't handle non-finite values.
Results may differ from a plain program's by a relative error of at most 0.0003.
Values sent between devices are 32-bit elements; how exact they have to be, the bound alone decides.
A program may use at most 128 MiB of HBM per device.

v0:
```python
import numpy as np
import jax
import jax.numpy as jnp
from jax import lax
from jax.experimental import pallas as pl
from jax.experimental.pallas import tpu as pltpu
from jax.sharding import PartitionSpec as P

HALF = 15
TAPS = 2 * HALF + 1
ORDERS = 5
NBASIS = 25
CELL = 64
STAMP = 32
ROWS = 64
PAD = 16
LANES = 128
SIGMA = 5.0
MESH = pl.DeviceIdType.MESH
F32 = jnp.float32
BF16 = jnp.bfloat16


def filter_bank():
    x = (np.arange(TAPS) - HALF) / SIGMA
    env = np.exp(-0.5 * x * x)
    poly = [
        np.ones_like(x),
        2.0 * x,
        4.0 * x**2 - 2.0,
        8.0 * x**3 - 12.0 * x,
        16.0 * x**4 - 48.0 * x**2 + 12.0,
    ]
    shaped = np.stack(poly) * env[None]
    return shaped / np.sqrt(np.sum(shaped * shaped, axis=1, keepdims=True))


def taps_at(filters, index):
    inside = (index >= 0) & (index < TAPS)
    return np.where(inside[None], filters[:, np.clip(index, 0, TAPS - 1)], 0.0)


def halves(values):
    values = np.asarray(values, np.float32)
    high = values.astype(BF16)
    low = (values - high.astype(np.float32)).astype(BF16)
    return [jnp.asarray(high), jnp.asarray(low)]


def constants(filters, cells):
    width = cells * CELL
    stamp_rows = taps_at(filters, np.arange(CELL)[None, :] - np.arange(STAMP)[:, None])
    stamp_rows = stamp_rows.reshape(ORDERS * STAMP, CELL)
    one = taps_at(filters, np.arange(CELL)[:, None] - np.arange(STAMP)[None, :])
    stamp_cols = np.zeros((4, CELL, ORDERS, 4, STAMP))
    for g in range(4):
        stamp_cols[g, :, :, g, :] = np.transpose(one, (1, 0, 2))
    stamp_cols = stamp_cols.reshape(4 * CELL, ORDERS * LANES)
    full_cols = taps_at(filters, np.arange(2 * LANES)[:, None] - np.arange(LANES)[None, :] - 1)
    full_cols = np.transpose(full_cols, (1, 0, 2)).reshape(2 * LANES, ORDERS * LANES)
    full_rows = taps_at(filters, np.arange(ROWS + 2 * PAD)[None, :] - np.arange(ROWS)[:, None] - 1)
    full_rows = np.transpose(full_rows, (1, 0, 2)).reshape(ROWS, ORDERS * (ROWS + 2 * PAD))
    lane_cell = np.arange(cells * STAMP)[:, None] // STAMP == np.arange(LANES)[None, :]
    cell_lane = np.arange(LANES)[:, None] == np.arange(width)[None, :] // CELL
    return (
        halves(stamp_rows)
        + halves(stamp_cols)
        + halves(full_cols)
        + halves(full_rows)
        + [jnp.asarray(lane_cell, BF16), jnp.asarray(cell_lane, BF16)]
    )


def dot(a, b):
    return jnp.dot(a, b, preferred_element_type=F32)


def split2(x):
    high = x.astype(BF16)
    return high, (x - high.astype(F32)).astype(BF16)


def split3(x):
    high = x.astype(BF16)
    rest = x - high.astype(F32)
    mid = rest.astype(BF16)
    return high, mid, (rest - mid.astype(F32)).astype(BF16)


def dot3(a, b):
    return dot(a[0], b[0]) + (dot(a[0], b[1]) + dot(a[1], b[0]))


def pick_sum(x, selector):
    high, mid, low = split3(x)
    return dot(high, selector) + (dot(mid, selector) + dot(low, selector))


def gather_kernel(counts, owner_ref, slot_ref, out_ref, ext, landed, rs_send, rs_recv, ag_send, ag_recv, ha_send, ha_recv):
    sky_count, visits, patches = counts
    sky = lax.axis_index("sky")
    visit = lax.axis_index("visit")
    patch = lax.axis_index("patch")
    chunk = ROWS // visits
    width = slot_ref.shape[1]
    full = width + 2 * LANES
    ways = [(ds, dp) for dp in (-1, 0, 1) for ds in (-1, 0, 1) if (ds, dp) != (0, 0)]

    def exists(ds, dp):
        return (sky + ds >= 0) & (sky + ds < sky_count) & (patch + dp >= 0) & (patch + dp < patches)

    def there(ds, dp):
        return {"sky": jnp.clip(sky + ds, 0, sky_count - 1), "patch": jnp.clip(patch + dp, 0, patches - 1)}

    ext[0:PAD, :] = jnp.zeros((PAD, full), F32)
    ext[PAD + ROWS :, :] = jnp.zeros((PAD, full), F32)
    ext[PAD : PAD + ROWS, 0:LANES] = jnp.zeros((ROWS, LANES), F32)
    ext[PAD : PAD + ROWS, full - LANES :] = jnp.zeros((ROWS, LANES), F32)

    barrier = pltpu.get_barrier_semaphore()
    for d in range(1, visits):
        pl.semaphore_signal(barrier, inc=1, device_id={"visit": lax.rem(visit + d, visits)}, device_id_type=MESH)
    total = jnp.int32(visits - 1)
    for ds, dp in ways:
        ok = exists(ds, dp)

        @pl.when(ok)
        def _():
            pl.semaphore_signal(barrier, inc=1, device_id=there(ds, dp), device_id_type=MESH)

        total = total + ok.astype(jnp.int32)
    pl.semaphore_wait(barrier, total)

    scatter = []
    for d in range(1, visits):
        to = lax.rem(visit + d, visits)
        copy = pltpu.make_async_remote_copy(
            src_ref=slot_ref.at[pl.ds(pl.multiple_of(to * chunk, chunk), chunk), :],
            dst_ref=landed.at[d - 1],
            send_sem=rs_send.at[d - 1],
            recv_sem=rs_recv.at[d - 1],
            device_id={"visit": to},
            device_id_type=MESH,
        )
        copy.start()
        scatter.append(copy)
    owner = owner_ref[0, 0]
    mine = slot_ref[pl.ds(pl.multiple_of(visit * chunk, chunk), chunk), :]
    current = jnp.where(owner == visit, mine, 0.0)
    for d in range(1, visits):
        scatter[d - 1].wait_recv()
        source = lax.rem(visit + visits - d, visits)
        current = jnp.where(owner == source, landed[d - 1], current)
    here = pl.ds(pl.multiple_of(PAD + visit * chunk, chunk), chunk)
    ext[here, LANES : LANES + width] = current
    gather = []
    for d in range(1, visits):
        copy = pltpu.make_async_remote_copy(
            src_ref=ext.at[here, pl.ds(LANES, width)],
            dst_ref=ext.at[here, pl.ds(LANES, width)],
            send_sem=ag_send.at[d - 1],
            recv_sem=ag_recv.at[d - 1],
            device_id={"visit": lax.rem(visit + d, visits)},
            device_id_type=MESH,
        )
        copy.start()
        gather.append(copy)
    for d in range(1, visits):
        source = lax.rem(visit + visits - d, visits)
        rows = pl.ds(pl.multiple_of(PAD + source * chunk, chunk), chunk)
        pltpu.make_async_remote_copy(
            src_ref=ext.at[rows, pl.ds(LANES, width)],
            dst_ref=ext.at[rows, pl.ds(LANES, width)],
            send_sem=ag_send.at[d - 1],
            recv_sem=ag_recv.at[d - 1],
            device_id={"visit": source},
            device_id_type=MESH,
        ).wait_recv()

    row_span = {-1: (PAD, PAD + ROWS, PAD), 0: (PAD, PAD, ROWS), 1: (ROWS, 0, PAD)}
    col_span = {-1: (LANES, LANES + width, LANES), 0: (LANES, LANES, width), 1: (width, 0, LANES)}
    edges = []
    for way, (ds, dp) in enumerate(ways):
        row_src, row_dst, row_len = row_span[dp]
        col_src, col_dst, col_len = col_span[ds]
        copy = pltpu.make_async_remote_copy(
            src_ref=ext.at[pl.ds(row_src, row_len), pl.ds(col_src, col_len)],
            dst_ref=ext.at[pl.ds(row_dst, row_len), pl.ds(col_dst, col_len)],
            send_sem=ha_send.at[way],
            recv_sem=ha_recv.at[way],
            device_id=there(ds, dp),
            device_id_type=MESH,
        )
        edges.append(copy)

        @pl.when(exists(ds, dp))
        def _():
            copy.start()

    for copy in scatter:
        copy.wait_send()
    for copy in gather:
        copy.wait_send()
    for way, (ds, dp) in enumerate(ways):

        @pl.when(exists(ds, dp))
        def _():
            edges[way].wait_send()

        @pl.when(exists(-ds, -dp))
        def _():
            edges[way].wait_recv()

    out_ref[...] = ext[...]


def gather_coadd(owner, slot, counts):
    visits = counts[1]
    width = slot.shape[1]
    dma = pltpu.SemaphoreType.DMA
    return pl.pallas_call(
        lambda *refs: gather_kernel(counts, *refs),
        name="gather_coadd",
        out_shape=jax.ShapeDtypeStruct((ROWS + 2 * PAD, width + 2 * LANES), F32),
        in_specs=[pl.BlockSpec(memory_space=pltpu.SMEM), pl.BlockSpec(memory_space=pltpu.VMEM)],
        out_specs=pl.BlockSpec(memory_space=pltpu.VMEM),
        scratch_shapes=[
            pltpu.VMEM((ROWS + 2 * PAD, width + 2 * LANES), F32),
            pltpu.VMEM((visits - 1, ROWS // visits, width), F32),
            dma((visits - 1,)),
            dma((visits - 1,)),
            dma((visits - 1,)),
            dma((visits - 1,)),
            dma((8,)),
            dma((8,)),
        ],
        compiler_params=pltpu.CompilerParams(collective_id=0, has_side_effects=True),
    )(owner, slot)


def eliminate(rows, flux):
    count = len(rows)
    starts = [8 * (k // 8) for k in range(count)]
    for j in range(count):
        first = 8 * (j // 8)
        for i in range(j):
            if starts[i] < first:
                rows[i] = rows[i][first - starts[i] :]
                starts[i] = first
        pivot_row = rows[j]
        scaled = pivot_row * (1.0 / pivot_row[j - first : j - first + 1])
        for i in range(count):
            if i < j:
                rows[i] = rows[i] - rows[i][j - first : j - first + 1] * scaled
            elif i > j:
                factor = pivot_row[i - first : i - first + 1]
                rows[i] = rows[i] - factor * scaled[starts[i] - first :]
        rows[j] = scaled
    weights = jnp.concatenate([row[1:2] for row in rows] + [jnp.zeros((7, LANES), F32)], axis=0)
    unit = jnp.concatenate([row[2:3] for row in rows] + [jnp.zeros((7, LANES), F32)], axis=0)
    return weights, unit


def solve_kernel(
    flux, offset_ref, ext_ref, image_ref,
    srow_h, srow_l, scol_h, scol_l, fcol_h, fcol_l, frow_h, frow_l, lane_cell, cell_lane,
    resid_ref, unit_ref, rows_ref, sum_ref,
    shifted, stamps, pairs, combined_h, combined_l,
):
    width = image_ref.shape[1]
    cells = width // CELL
    full = width + 2 * LANES
    ext_rows = ROWS + 2 * PAD
    shifted[0:ext_rows, :] = pltpu.roll(ext_ref[...], full - (LANES - PAD), 1)
    shifted[ext_rows:, :] = jnp.zeros((8, full), F32)

    lane = lax.broadcasted_iota(jnp.int32, (CELL, LANES), 1)
    windows = []
    for h in range(cells // 2):
        parts = []
        for odd in range(2):
            g = 2 * h + odd
            block = shifted[:, LANES * h : LANES * h + 2 * LANES]
            block = pltpu.roll(block, ext_rows + 7 - offset_ref[0, g], 0)[0:CELL]
            move = 2 * LANES - offset_ref[1, g] - 1
            parts.append(pltpu.roll(block, move, 1)[:, 0:LANES])
        windows.append(jnp.where(lane < CELL, parts[0], parts[1]))
    window = jnp.concatenate(windows, axis=1)
    rows_done = dot3((srow_h[...], srow_l[...]), split2(window))
    groups = cells // 4
    stacked = jnp.concatenate([rows_done[:, 4 * CELL * q : 4 * CELL * (q + 1)] for q in range(groups)], axis=0)
    basis = dot3(split2(stacked), (scol_h[...], scol_l[...]))
    for q in range(groups):
        for b in range(ORDERS):
            first = (q * ORDERS + b) * STAMP
            for a in range(ORDERS):
                stamps[ORDERS * a + b, :, LANES * q : LANES * (q + 1)] = basis[first : first + STAMP, LANES * a : LANES * (a + 1)]
    lane = lax.broadcasted_iota(jnp.int32, (STAMP, LANES), 1)
    for q in range(groups):
        merged = jnp.zeros((STAMP, LANES), F32)
        for inner in range(4):
            g = 4 * q + inner
            first = LANES * (g // 2)
            block = image_ref[:, first : first + LANES]
            block = pltpu.roll(block, lax.rem(ROWS - offset_ref[0, g], ROWS), 0)[0:STAMP]
            move = lax.rem(2 * LANES + STAMP * inner - CELL * (g % 2) - offset_ref[1, g], LANES)
            merged = jnp.where(lane // STAMP == inner, pltpu.roll(block, move, 1), merged)
        stamps[NBASIS, :, LANES * q : LANES * (q + 1)] = merged
    for spare in range(NBASIS + 1, 32):
        stamps[spare] = jnp.zeros((STAMP, cells * STAMP), F32)

    spots = []
    at = 0
    for k in range(NBASIS):
        low = 8 * (k // 8)
        mine = stamps[k]
        for tile in range(low, 32, 8):
            pairs[at + tile - low : at + tile - low + 8, :] = jnp.sum(stamps[tile : tile + 8] * mine[None], axis=1)
        spots.append((at, 32 - low))
        at += 32 - low
    sums = pick_sum(pairs[...], lane_cell[...])
    rows = []
    for k, (at, length) in enumerate(spots):
        row = sums[at : at + length]
        place = lax.broadcasted_iota(jnp.int32, row.shape, 0) + (32 - length)
        row = jnp.where(place == NBASIS + 1, float(flux[k]), row)
        rows.append(row)
    padding = lax.broadcasted_iota(jnp.int32, (1, LANES), 1) >= cells
    diag = []
    for k, (at, length) in enumerate(spots):
        place = lax.broadcasted_iota(jnp.int32, rows[k].shape, 0) + (32 - length)
        diag.append(jnp.where(padding & (place == k), 1.0, rows[k]))
    weights, unit = eliminate(diag, flux)

    flux_col = jnp.concatenate([jnp.full((1, LANES), float(f), F32) for f in flux] + [jnp.zeros((7, LANES), F32)], axis=0)
    flux_cells = jnp.sum(weights * flux_col, axis=0, keepdims=True)
    curve_cells = jnp.sum(unit * flux_col, axis=0, keepdims=True)
    both = jnp.concatenate([flux_cells, curve_cells, jnp.zeros((6, LANES), F32)], axis=0)
    spread = pick_sum(jnp.concatenate([weights, unit, both], axis=0), cell_lane[...])
    rows_ref[...] = spread[64:72]
    local = jnp.sum(jnp.where(padding, 0.0, flux_cells), axis=1, keepdims=True)
    sum_ref[...] = jnp.broadcast_to(local, (8, LANES))

    blocks = width // LANES
    windows = jnp.concatenate(
        [shifted[0:ext_rows, LANES * h : LANES * h + 2 * LANES] for h in range(blocks)], axis=0
    )
    columns = dot3(split2(windows), (fcol_h[...], fcol_l[...]))
    for which in range(2):
        for h in range(blocks):
            for b in range(ORDERS):
                acc = None
                for a in range(ORDERS):
                    k = 32 * which + ORDERS * a + b
                    term = spread[k : k + 1, LANES * h : LANES * (h + 1)] * columns[
                        ext_rows * h : ext_rows * (h + 1), LANES * a : LANES * (a + 1)
                    ]
                    acc = term if acc is None else acc + term
                high, low = split2(acc)
                spot = (slice(ext_rows * b, ext_rows * (b + 1)), slice(width * which + LANES * h, width * which + LANES * (h + 1)))
                combined_h[spot] = high
                combined_l[spot] = low
    matched = dot3((frow_h[...], frow_l[...]), (combined_h[...], combined_l[...]))
    resid_ref[...] = image_ref[...] - matched[:, 0:width]
    unit_ref[...] = matched[:, width:]


def solve_cells(offsets, ext, image, filters):
    width = image.shape[1]
    cells = width // CELL
    sums = filters.sum(axis=1)
    flux = (sums[:, None] * sums[None, :]).reshape(-1)
    consts = constants(filters, cells)
    pair_rows = sum(32 - 8 * (k // 8) for k in range(NBASIS))
    vmem = pl.BlockSpec(memory_space=pltpu.VMEM)
    deep = ORDERS * (ROWS + 2 * PAD)
    return pl.pallas_call(
        lambda *refs: solve_kernel(flux, *refs),
        name="solve_cells",
        out_shape=[
            jax.ShapeDtypeStruct((ROWS, width), F32),
            jax.ShapeDtypeStruct((ROWS, width), F32),
            jax.ShapeDtypeStruct((8, width), F32),
            jax.ShapeDtypeStruct((8, LANES), F32),
        ],
        in_specs=[pl.BlockSpec(memory_space=pltpu.SMEM)] + [vmem] * (2 + len(consts)),
        out_specs=[vmem] * 4,
        scratch_shapes=[
            pltpu.VMEM((ROWS + 2 * PAD + 8, width + 2 * LANES), F32),
            pltpu.VMEM((32, STAMP, cells * STAMP), F32),
            pltpu.VMEM((pair_rows, cells * STAMP), F32),
            pltpu.VMEM((deep, 2 * width), BF16),
            pltpu.VMEM((deep, 2 * width), BF16),
        ],
        compiler_params=pltpu.CompilerParams(vmem_limit_bytes=48 << 20),
    )(offsets, ext, image, *consts)


def exchange_kernel(counts, mine_ref, out_ref, landed, send, recv):
    sky_count, _, patches = counts
    members = sky_count * patches
    me = lax.axis_index("sky") * patches + lax.axis_index("patch")

    def device(d):
        other = lax.rem(me + d, members)
        return {"sky": other // patches, "patch": lax.rem(other, patches)}

    barrier = pltpu.get_barrier_semaphore()
    for d in range(1, members):
        pl.semaphore_signal(barrier, inc=1, device_id=device(d), device_id_type=MESH)
    pl.semaphore_wait(barrier, members - 1)
    copies = []
    for d in range(1, members):
        copy = pltpu.make_async_remote_copy(
            src_ref=mine_ref,
            dst_ref=landed.at[d - 1],
            send_sem=send.at[d - 1],
            recv_sem=recv.at[d - 1],
            device_id=device(d),
            device_id_type=MESH,
        )
        copy.start()
        copies.append(copy)
    total = mine_ref[...]
    for d in range(1, members):
        copies[d - 1].wait_recv()
        total = total + landed[d - 1]
    for copy in copies:
        copy.wait_send()
    out_ref[...] = total


def exchange_sums(value, counts):
    members = counts[0] * counts[2]
    vmem = pl.BlockSpec(memory_space=pltpu.VMEM)
    return pl.pallas_call(
        lambda *refs: exchange_kernel(counts, *refs),
        name="exchange_sums",
        out_shape=jax.ShapeDtypeStruct(value.shape, F32),
        in_specs=[vmem],
        out_specs=vmem,
        scratch_shapes=[
            pltpu.VMEM((members - 1,) + value.shape, F32),
            pltpu.SemaphoreType.DMA((members - 1,)),
            pltpu.SemaphoreType.DMA((members - 1,)),
        ],
        compiler_params=pltpu.CompilerParams(collective_id=1, has_side_effects=True),
    )(value)


def solution(mesh):
    counts = (mesh.shape["sky"], mesh.shape["visit"], mesh.shape["patch"])
    filters = filter_bank()

    def body(template_store, science, owner_visit, stamp_offset):
        ext = gather_coadd(owner_visit, template_store[0], counts)
        resid, unit, rows, local = solve_cells(stamp_offset[:, 0, 0, :], ext, science[0], filters)
        total = exchange_sums(local, counts)
        stamps = science.shape[2] // CELL * counts[0] * counts[2]
        mean_flux = total[0:1, 0:1] / stamps
        correction = (mean_flux - rows[0:1]) / rows[1:2]
        return (resid - correction * unit)[None]

    spec = P("visit", "patch", "sky")
    in_specs = (spec, spec, P("sky", "patch"), P(None, "visit", "patch", "sky"))
    return jax.shard_map(body, mesh=mesh, in_specs=in_specs, out_specs=spec, check_vma=False)
```

profile of v0, /device:TPU:0, one launch (start us, length us, event | category | flops | bytes accessed | tf_op | source)
XLA Modules:
  0.0 43.6 jit_solution(6477124759291909060)
XLA Ops:
  0.0 0.0 copy-start.1
  0.7 0.0 copy-start.7
  0.7 0.0 copy-start.10
  0.7 0.0 copy-start.13
  0.7 18.8 %gather_coadd.1.refs_1_ = f32[96,768]{1,0:T(8,128)} custom-call(s32[1,1]{1,0:T(1,128)S(6)} %copy.15.refs_0_, f32[64,512]{1,0:T(8,128)} %bitcast.9), custom_call_target="tpu_custom_call" | custom-call | tf_op jit(solution)/shard_map/gather_coadd/pallas_call | solution.py:221
  19.6 0.0 copy-done.1
  19.6 0.0 copy-done.7
  19.6 0.0 copy-done.10
  19.6 0.0 copy-done.13
  19.6 0.0 copy-start
  19.6 1.0 %copy-done = f32[96,768]{1,0:T(8,128)S(1)} copy-done((f32[96,768]{1,0:T(8,128)S(1)}, f32[96,768]{1,0:T(8,128)}, u32[]{:S(2)}) %copy-start) | copy-done | bytes 294936
  20.6 0.0 copy-start.2
  20.6 1.0 %copy-done.2 = bf16[256,640]{1,0:T(8,128)(2,1)S(1)} copy-done((bf16[256,640]{1,0:T(8,128)(2,1)S(1)}, bf16[256,640]{1,0:T(8,128)(2,1)}, u32[]{:S(2)}) %copy-start.2) | copy-done | bytes 327704
  21.6 0.0 copy-start.3
  21.6 1.0 %copy-done.3 = bf16[256,640]{1,0:T(8,128)(2,1)S(1)} copy-done((bf16[256,640]{1,0:T(8,128)(2,1)S(1)}, bf16[256,640]{1,0:T(8,128)(2,1)}, u32[]{:S(2)}) %copy-start.3) | copy-done | bytes 327704
  22.5 0.0 copy-start.4
  22.5 1.0 %copy-done.4 = bf16[256,640]{1,0:T(8,128)(2,1)S(1)} copy-done((bf16[256,640]{1,0:T(8,128)(2,1)S(1)}, bf16[256,640]{1,0:T(8,128)(2,1)}, u32[]{:S(2)}) %copy-start.4) | copy-done | bytes 327704
  23.5 0.0 copy-start.5
  23.5 0.9 %copy-done.5 = f32[1,64,512]{2,1,0:T(8,128)S(1)} copy-done((f32[1,64,512]{2,1,0:T(8,128)S(1)}, f32[1,64,512]{2,1,0:T(8,128)}, u32[]{:S(2)}) %copy-start.5) | copy-done | bytes 131096
  24.4 0.9 %copy-done.6 = bf16[128,512]{1,0:T(8,128)(2,1)S(1)} copy-done((bf16[128,512]{1,0:T(8,128)(2,1)S(1)}, bf16[128,512]{1,0:T(8,128)(2,1)}, u32[]{:S(2)}) %copy-start.6) | copy-done | bytes 131096
  25.3 0.0 copy-start.8
  25.3 0.8 %copy-done.8 = bf16[64,480]{1,0:T(8,128)(2,1)S(1)} copy-done((bf16[64,480]{1,0:T(8,128)(2,1)S(1)}, bf16[64,480]{1,0:T(8,128)(2,1)}, u32[]{:S(2)}) %copy-start.8) | copy-done | bytes 61464
  26.2 0.0 copy-start.9
  26.2 0.8 %copy-done.9 = bf16[64,480]{1,0:T(8,128)(2,1)S(1)} copy-done((bf16[64,480]{1,0:T(8,128)(2,1)S(1)}, bf16[64,480]{1,0:T(8,128)(2,1)}, u32[]{:S(2)}) %copy-start.9) | copy-done | bytes 61464
  27.0 0.0 copy-start.11
  27.0 0.8 %copy-done.11 = bf16[160,64]{1,0:T(8,128)(2,1)S(1)} copy-done((bf16[160,64]{1,0:T(8,128)(2,1)S(1)}, bf16[160,64]{1,0:T(8,128)(2,1)}, u32[]{:S(2)}) %copy-start.11) | copy-done | bytes 20504
  27.8 6.3 %solve_cells.1 = (f32[64,512]{1,0:T(8,128)S(1)}, f32[64,512]{1,0:T(8,128)S(1)}, f32[8,512]{1,0:T(8,128)S(1)}, f32[8,128]{1,0:T(8,128)S(1)}) custom-call(s32[2,8]{1,0:T(2,128)S(1)} %bitcast.8, f32[96,768]{1,0:T(8,128)S(1)} %copy-done, f32[64,512]{1,0:T(8,128)S(1)} %bitcast.7, bf16[160,64]{1,0:T(8,128)(2,1)S(1)} %copy-done.11, bf16[160,64]{1,0:T(8,128)(2,1)S(1)} %copy-done.10, ...), custom_call_target="tpu_custom_call" | custom-call | tf_op jit(solution)/shard_map/solve_cells/pallas_call | solution.py:377
  34.1 0.0 copy-start.12
  34.1 0.6 %copy-done.12 = f32[8,128]{1,0:T(8,128)} copy-done((f32[8,128]{1,0:T(8,128)}, f32[8,128]{1,0:T(8,128)S(1)}, u32[]{:S(2)}) %copy-start.12) | copy-done | bytes 4120
  34.7 6.4 %exchange_sums.1 = f32[8,128]{1,0:T(8,128)} custom-call(f32[8,128]{1,0:T(8,128)} %copy-done.12), custom_call_target="tpu_custom_call" | custom-call | tf_op jit(solution)/shard_map/exchange_sums/pallas_call | solution.py:436
  41.0 1.2 %slice.9 = f32[1,1]{1,0:T(1,128)} slice(f32[8,128]{1,0:T(8,128)} %exchange_sums.1), slice={[0:1], [0:1]} | slice | bytes 8 | tf_op jit(solution)/shard_map/slice | solution.py:460
  42.9 0.7 %subtract_bitcast_fusion = f32[1,64,512]{2,1,0:T(8,128)} fusion(f32[64,512]{1,0:T(8,128)S(1)} %get-tuple-element.9, f32[64,512]{1,0:T(8,128)S(1)} %get-tuple-element.12, f32[512]{0:T(512)S(1)} %bitcast.10), kind=kLoop, calls=%fused_computation | loop fusion | flops 65536 | bytes 395264 | tf_op jit(solution)/shard_map/broadcast_in_dim | solution.py:462
  (2 shorter events, 0.0 us)
Async XLA Ops:
  0.0 19.6 %copy-start.1 = (bf16[256,640]{1,0:T(8,128)(2,1)S(1)}, bf16[256,640]{1,0:T(8,128)(2,1)}, u32[]{:S(2)}) copy-start(bf16[256,640]{1,0:T(8,128)(2,1)} %constant.28.clone.refs_8_) | copy-start | bytes 983044
  0.7 18.9 %copy-start.7 = (bf16[256,128]{1,0:T(8,128)(2,1)S(1)}, bf16[256,128]{1,0:T(8,128)(2,1)}, u32[]{:S(2)}) copy-start(bf16[256,128]{1,0:T(8,128)(2,1)} %constant.31.clone.refs_11_) | copy-start | bytes 196612
  0.7 18.9 %copy-start.10 = (bf16[160,64]{1,0:T(8,128)(2,1)S(1)}, bf16[160,64]{1,0:T(8,128)(2,1)}, u32[]{:S(2)}) copy-start(bf16[160,64]{1,0:T(8,128)(2,1)} %constant.24.clone.refs_4_) | copy-start | bytes 61444
  0.7 18.9 %copy-start.13 = (s32[2,1,1,8]{3,2,1,0:T(1,128)S(1)}, s32[2,1,1,8]{3,2,1,0:T(1,128)}, u32[]{:S(2)}) copy-start(s32[2,1,1,8]{3,2,1,0:T(1,128)} %param.17) | copy-start | bytes 196
  19.6 1.0 %copy-start = (f32[96,768]{1,0:T(8,128)S(1)}, f32[96,768]{1,0:T(8,128)}, u32[]{:S(2)}) copy-start(f32[96,768]{1,0:T(8,128)} %gather_coadd.1.refs_1_) | copy-start | bytes 884740
  20.6 1.0 %copy-start.2 = (bf16[256,640]{1,0:T(8,128)(2,1)S(1)}, bf16[256,640]{1,0:T(8,128)(2,1)}, u32[]{:S(2)}) copy-start(bf16[256,640]{1,0:T(8,128)(2,1)} %constant.27.clone.refs_7_) | copy-start | bytes 983044
  21.6 1.0 %copy-start.3 = (bf16[256,640]{1,0:T(8,128)(2,1)S(1)}, bf16[256,640]{1,0:T(8,128)(2,1)}, u32[]{:S(2)}) copy-start(bf16[256,640]{1,0:T(8,128)(2,1)} %constant.26.clone.refs_6_) | copy-start | bytes 983044
  22.5 1.0 %copy-start.4 = (bf16[256,640]{1,0:T(8,128)(2,1)S(1)}, bf16[256,640]{1,0:T(8,128)(2,1)}, u32[]{:S(2)}) copy-start(bf16[256,640]{1,0:T(8,128)(2,1)} %constant.25.clone.refs_5_) | copy-start | bytes 983044
  23.5 0.9 %copy-start.5 = (f32[1,64,512]{2,1,0:T(8,128)S(1)}, f32[1,64,512]{2,1,0:T(8,128)}, u32[]{:S(2)}) copy-start(f32[1,64,512]{2,1,0:T(8,128)} %param.15) | copy-start | bytes 393220
  24.4 0.9 %copy-start.6 = (bf16[128,512]{1,0:T(8,128)(2,1)S(1)}, bf16[128,512]{1,0:T(8,128)(2,1)}, u32[]{:S(2)}) copy-start(bf16[128,512]{1,0:T(8,128)(2,1)} %constant.32.clone.refs_12_) | copy-start | bytes 393220
  25.3 0.8 %copy-start.8 = (bf16[64,480]{1,0:T(8,128)(2,1)S(1)}, bf16[64,480]{1,0:T(8,128)(2,1)}, u32[]{:S(2)}) copy-start(bf16[64,480]{1,0:T(8,128)(2,1)} %constant.30.clone.refs_10_) | copy-start | bytes 184324
  26.2 0.8 %copy-start.9 = (bf16[64,480]{1,0:T(8,128)(2,1)S(1)}, bf16[64,480]{1,0:T(8,128)(2,1)}, u32[]{:S(2)}) copy-start(bf16[64,480]{1,0:T(8,128)(2,1)} %constant.29.clone.refs_9_) | copy-start | bytes 184324
  27.0 0.8 %copy-start.11 = (bf16[160,64]{1,0:T(8,128)(2,1)S(1)}, bf16[160,64]{1,0:T(8,128)(2,1)}, u32[]{:S(2)}) copy-start(bf16[160,64]{1,0:T(8,128)(2,1)} %constant.23.clone.refs_3_) | copy-start | bytes 61444
  34.1 0.6 %copy-start.12 = (f32[8,128]{1,0:T(8,128)}, f32[8,128]{1,0:T(8,128)S(1)}, u32[]{:S(2)}) copy-start(f32[8,128]{1,0:T(8,128)S(1)} %get-tuple-element.10.refs_0_) | copy-start | bytes 12292
where the time goes:
time: 44.1 us; the launch traced here: 43.6 us
  Pallas kernels  31.5 us (71%)
  local copies, waits for them, and re-layouts  9.93 us (23%)
  between operations  1.46 us (3%)
  other arithmetic  0.68 us (2%)
    pallas_call x1, Pallas kernels, gather_coadd(): pl.pallas_call(lambda *refs: gather_kernel(counts, *refs), name='gather_c...  18.8 us
    unnamed x28, local copies, waits for them, and re-layouts  8.74 us
    pallas_call x1, Pallas kernels, exchange_sums(): pl.pallas_call(lambda *refs: exchange_kernel(counts, *refs), name='exchan...  6.36 us
    pallas_call x1, Pallas kernels, solve_cells(): pl.pallas_call(lambda *refs: solve_kernel(flux, *refs), name='solve_cells...  6.28 us
    slice x1, local copies, waits for them, and re-layouts, body(): mean_flux = total[0:1, 0:1] / stamps  1.19 us

commit v1 on v0

v1 whole, which is shorter than its diff:
```python
import numpy as np
import jax
import jax.numpy as jnp
from jax import lax
from jax.experimental import pallas as pl
from jax.experimental.pallas import tpu as pltpu
from jax.sharding import PartitionSpec as P

HALF = 15
TAPS = 2 * HALF + 1
ORDERS = 5
NBASIS = 25
CELL = 64
STAMP = 32
ROWS = 64
PAD = 16
LANES = 128
SIGMA = 5.0
MESH = pl.DeviceIdType.MESH
F32 = jnp.float32
BF16 = jnp.bfloat16


def filter_bank():
    x = (np.arange(TAPS) - HALF) / SIGMA
    env = np.exp(-0.5 * x * x)
    poly = [
        np.ones_like(x),
        2.0 * x,
        4.0 * x**2 - 2.0,
        8.0 * x**3 - 12.0 * x,
        16.0 * x**4 - 48.0 * x**2 + 12.0,
    ]
    shaped = np.stack(poly) * env[None]
    return shaped / np.sqrt(np.sum(shaped * shaped, axis=1, keepdims=True))


def taps_at(filters, index):
    inside = (index >= 0) & (index < TAPS)
    return np.where(inside[None], filters[:, np.clip(index, 0, TAPS - 1)], 0.0)


def halves(values):
    values = np.asarray(values, np.float32)
    high = values.astype(BF16)
    low = (values - high.astype(np.float32)).astype(BF16)
    return [jnp.asarray(np.stack([high, low]))]


def constants(filters, cells):
    width = cells * CELL
    stamp_rows = taps_at(filters, np.arange(CELL)[None, :] - np.arange(STAMP)[:, None])
    stamp_rows = stamp_rows.reshape(ORDERS * STAMP, CELL)
    one = taps_at(filters, np.arange(CELL)[:, None] - np.arange(STAMP)[None, :])
    stamp_cols = np.zeros((4, CELL, ORDERS, 4, STAMP))
    for g in range(4):
        stamp_cols[g, :, :, g, :] = np.transpose(one, (1, 0, 2))
    stamp_cols = stamp_cols.reshape(4 * CELL, ORDERS * LANES)
    full_cols = taps_at(filters, np.arange(2 * LANES)[:, None] - np.arange(LANES)[None, :] - 1)
    full_cols = np.transpose(full_cols, (1, 0, 2)).reshape(2 * LANES, ORDERS * LANES)
    full_rows = taps_at(filters, np.arange(ROWS + 2 * PAD)[None, :] - np.arange(ROWS)[:, None] - 1)
    full_rows = np.transpose(full_rows, (1, 0, 2)).reshape(ROWS, ORDERS * (ROWS + 2 * PAD))
    lane_cell = np.arange(cells * STAMP)[:, None] // STAMP == np.arange(LANES)[None, :]
    cell_lane = np.arange(LANES)[:, None] == np.arange(width)[None, :] // CELL
    return (
        halves(stamp_rows)
        + halves(stamp_cols)
        + halves(full_cols)
        + halves(full_rows)
        + [jnp.asarray(lane_cell, BF16), jnp.asarray(cell_lane, BF16)]
    )


def dot(a, b):
    return jnp.dot(a, b, preferred_element_type=F32)


def split2(x):
    high = x.astype(BF16)
    return high, (x - high.astype(F32)).astype(BF16)


def split3(x):
    high = x.astype(BF16)
    rest = x - high.astype(F32)
    mid = rest.astype(BF16)
    return high, mid, (rest - mid.astype(F32)).astype(BF16)


def dot3(a, b):
    return dot(a[0], b[0]) + (dot(a[0], b[1]) + dot(a[1], b[0]))


def pick_sum(x, selector):
    high, mid, low = split3(x)
    return dot(high, selector) + (dot(mid, selector) + dot(low, selector))


def eliminate(rows, flux):
    count = len(rows)
    starts = [8 * (k // 8) for k in range(count)]
    for j in range(count):
        first = 8 * (j // 8)
        for i in range(j):
            if starts[i] < first:
                rows[i] = rows[i][first - starts[i] :]
                starts[i] = first
        pivot_row = rows[j]
        scaled = pivot_row * (1.0 / pivot_row[j - first : j - first + 1])
        for i in range(count):
            if i < j:
                rows[i] = rows[i] - rows[i][j - first : j - first + 1] * scaled
            elif i > j:
                factor = pivot_row[i - first : i - first + 1]
                rows[i] = rows[i] - factor * scaled[starts[i] - first :]
        rows[j] = scaled
    weights = jnp.concatenate([row[1:2] for row in rows] + [jnp.zeros((7, LANES), F32)], axis=0)
    unit = jnp.concatenate([row[2:3] for row in rows] + [jnp.zeros((7, LANES), F32)], axis=0)
    return weights, unit


def fused_kernel(
    counts, flux, owner_hbm, offset_hbm, slot_hbm, image_hbm,
    srow_hbm, scol_hbm, fcol_hbm, frow_hbm, pick_hbm, put_hbm,
    out_ref,
    owner_ref, offset_ref, mine_ref, image_ref, srow, scol, fcol, frow, lane_cell, cell_lane,
    ext, landed, shifted, stamps, pairs, combined_h, combined_l, sum_ref, sum_landed,
    local_sem, rs_send, rs_recv, ag_send, ag_recv, ha_send, ha_recv, fx_send, fx_recv,
):
    sky_count, visits, patches = counts
    members = sky_count * patches
    sky = lax.axis_index("sky")
    visit = lax.axis_index("visit")
    patch = lax.axis_index("patch")
    me = sky * patches + patch
    chunk = ROWS // visits
    width = image_ref.shape[1]
    cells = width // CELL
    full = width + 2 * LANES
    ext_rows = ROWS + 2 * PAD
    ways = [(ds, dp) for dp in (-1, 0, 1) for ds in (-1, 0, 1) if (ds, dp) != (0, 0)]

    def exists(ds, dp):
        return (sky + ds >= 0) & (sky + ds < sky_count) & (patch + dp >= 0) & (patch + dp < patches)

    def there(ds, dp):
        return {"sky": jnp.clip(sky + ds, 0, sky_count - 1), "patch": jnp.clip(patch + dp, 0, patches - 1)}

    def member(d):
        other = lax.rem(me + d, members)
        return {"sky": other // patches, "patch": lax.rem(other, patches)}

    own_rows = pl.ds(pl.multiple_of(visit * chunk, chunk), chunk)
    moves = [
        (owner_hbm, owner_ref),
        (offset_hbm, offset_ref),
        (slot_hbm.at[0, own_rows, :], mine_ref),
        (image_hbm.at[0], image_ref),
        (srow_hbm, srow),
        (scol_hbm, scol),
        (fcol_hbm, fcol),
        (frow_hbm, frow),
        (pick_hbm, lane_cell),
        (put_hbm, cell_lane),
    ]
    loads = [pltpu.make_async_copy(src, dst, local_sem.at[i]) for i, (src, dst) in enumerate(moves)]

    ext[0:PAD, :] = jnp.zeros((PAD, full), F32)
    ext[PAD + ROWS :, :] = jnp.zeros((PAD, full), F32)
    ext[PAD : PAD + ROWS, 0:LANES] = jnp.zeros((ROWS, LANES), F32)
    ext[PAD : PAD + ROWS, full - LANES :] = jnp.zeros((ROWS, LANES), F32)

    barrier = pltpu.get_barrier_semaphore()
    for d in range(1, visits):
        pl.semaphore_signal(barrier, inc=1, device_id={"visit": lax.rem(visit + d, visits)}, device_id_type=MESH)
    for d in range(1, members):
        pl.semaphore_signal(barrier, inc=1, device_id=member(d), device_id_type=MESH)
    for load in loads:
        load.start()
    pl.semaphore_wait(barrier, visits - 1 + members - 1)

    scatter = []
    for d in range(1, visits):
        to = lax.rem(visit + d, visits)
        copy = pltpu.make_async_remote_copy(
            src_ref=slot_hbm.at[0, pl.ds(pl.multiple_of(to * chunk, chunk), chunk), :],
            dst_ref=landed.at[d - 1],
            send_sem=rs_send.at[d - 1],
            recv_sem=rs_recv.at[d - 1],
            device_id={"visit": to},
            device_id_type=MESH,
        )
        copy.start()
        scatter.append(copy)
    for load in loads:
        load.wait()
    groups = cells // 4
    lane = lax.broadcasted_iota(jnp.int32, (STAMP, LANES), 1)
    for q in range(groups):
        merged = jnp.zeros((STAMP, LANES), F32)
        for inner in range(4):
            g = 4 * q + inner
            first = LANES * (g // 2)
            block = image_ref[:, first : first + LANES]
            block = pltpu.roll(block, lax.rem(ROWS - offset_ref[0, 0, 0, g], ROWS), 0)[0:STAMP]
            move = lax.rem(2 * LANES + STAMP * inner - CELL * (g % 2) - offset_ref[1, 0, 0, g], LANES)
            merged = jnp.where(lane // STAMP == inner, pltpu.roll(block, move, 1), merged)
        stamps[NBASIS, :, LANES * q : LANES * (q + 1)] = merged
    for spare in range(NBASIS + 1, 32):
        stamps[spare] = jnp.zeros((STAMP, cells * STAMP), F32)

    owner = owner_ref[0, 0]
    current = jnp.where(owner == visit, mine_ref[...], 0.0)
    for d in range(1, visits):
        scatter[d - 1].wait_recv()
        source = lax.rem(visit + visits - d, visits)
        current = jnp.where(owner == source, landed[d - 1], current)
    here = pl.ds(pl.multiple_of(PAD + visit * chunk, chunk), chunk)
    ext[here, LANES : LANES + width] = current
    gather = []
    for d in range(1, visits):
        copy = pltpu.make_async_remote_copy(
            src_ref=ext.at[here, pl.ds(LANES, width)],
            dst_ref=ext.at[here, pl.ds(LANES, width)],
            send_sem=ag_send.at[d - 1],
            recv_sem=ag_recv.at[d - 1],
            device_id={"visit": lax.rem(visit + d, visits)},
            device_id_type=MESH,
        )
        copy.start()
        gather.append(copy)
    for d in range(1, visits):
        source = lax.rem(visit + visits - d, visits)
        rows = pl.ds(pl.multiple_of(PAD + source * chunk, chunk), chunk)
        pltpu.make_async_remote_copy(
            src_ref=ext.at[rows, pl.ds(LANES, width)],
            dst_ref=ext.at[rows, pl.ds(LANES, width)],
            send_sem=ag_send.at[d - 1],
            recv_sem=ag_recv.at[d - 1],
            device_id={"visit": source},
            device_id_type=MESH,
        ).wait_recv()

    row_span = {-1: (PAD, PAD + ROWS, PAD), 0: (PAD, PAD, ROWS), 1: (ROWS, 0, PAD)}
    col_span = {-1: (LANES, LANES + width, LANES), 0: (LANES, LANES, width), 1: (width, 0, LANES)}
    edges = []
    for way, (ds, dp) in enumerate(ways):
        row_src, row_dst, row_len = row_span[dp]
        col_src, col_dst, col_len = col_span[ds]
        copy = pltpu.make_async_remote_copy(
            src_ref=ext.at[pl.ds(row_src, row_len), pl.ds(col_src, col_len)],
            dst_ref=ext.at[pl.ds(row_dst, row_len), pl.ds(col_dst, col_len)],
            send_sem=ha_send.at[way],
            recv_sem=ha_recv.at[way],
            device_id=there(ds, dp),
            device_id_type=MESH,
        )
        edges.append(copy)

        @pl.when(exists(ds, dp))
        def _():
            copy.start()

    for copy in scatter:
        copy.wait_send()
    for copy in gather:
        copy.wait_send()
    for way, (ds, dp) in enumerate(ways):

        @pl.when(exists(ds, dp))
        def _():
            edges[way].wait_send()

        @pl.when(exists(-ds, -dp))
        def _():
            edges[way].wait_recv()

    shifted[0:ext_rows, :] = pltpu.roll(ext[...], full - (LANES - PAD), 1)
    shifted[ext_rows:, :] = jnp.zeros((8, full), F32)

    lane = lax.broadcasted_iota(jnp.int32, (CELL, LANES), 1)
    windows = []
    for h in range(cells // 2):
        parts = []
        for odd in range(2):
            g = 2 * h + odd
            block = shifted[:, LANES * h : LANES * h + 2 * LANES]
            block = pltpu.roll(block, ext_rows + 7 - offset_ref[0, 0, 0, g], 0)[0:CELL]
            move = 2 * LANES - offset_ref[1, 0, 0, g] - 1
            parts.append(pltpu.roll(block, move, 1)[:, 0:LANES])
        windows.append(jnp.where(lane < CELL, parts[0], parts[1]))
    window = jnp.concatenate(windows, axis=1)
    rows_done = dot3((srow[0], srow[1]), split2(window))
    stacked = jnp.concatenate([rows_done[:, 4 * CELL * q : 4 * CELL * (q + 1)] for q in range(groups)], axis=0)
    basis = dot3(split2(stacked), (scol[0], scol[1]))
    for q in range(groups):
        for b in range(ORDERS):
            first = (q * ORDERS + b) * STAMP
            for a in range(ORDERS):
                stamps[ORDERS * a + b, :, LANES * q : LANES * (q + 1)] = basis[first : first + STAMP, LANES * a : LANES * (a + 1)]
    spots = []
    at = 0
    for k in range(NBASIS):
        low = 8 * (k // 8)
        mine = stamps[k]
        for tile in range(low, 32, 8):
            pairs[at + tile - low : at + tile - low + 8, :] = jnp.sum(stamps[tile : tile + 8] * mine[None], axis=1)
        spots.append((at, 32 - low))
        at += 32 - low
    sums = pick_sum(pairs[...], lane_cell[...])
    rows = []
    for k, (at, length) in enumerate(spots):
        row = sums[at : at + length]
        place = lax.broadcasted_iota(jnp.int32, row.shape, 0) + (32 - length)
        row = jnp.where(place == NBASIS + 1, float(flux[k]), row)
        rows.append(row)
    padding = lax.broadcasted_iota(jnp.int32, (1, LANES), 1) >= cells
    diag = []
    for k, (at, length) in enumerate(spots):
        place = lax.broadcasted_iota(jnp.int32, rows[k].shape, 0) + (32 - length)
        diag.append(jnp.where(padding & (place == k), 1.0, rows[k]))
    weights, unit = eliminate(diag, flux)

    flux_col = jnp.concatenate([jnp.full((1, LANES), float(f), F32) for f in flux] + [jnp.zeros((7, LANES), F32)], axis=0)
    flux_cells = jnp.sum(weights * flux_col, axis=0, keepdims=True)
    curve_cells = jnp.sum(unit * flux_col, axis=0, keepdims=True)
    local = jnp.sum(jnp.where(padding, 0.0, flux_cells), axis=1, keepdims=True)
    sum_ref[...] = jnp.broadcast_to(local, (8, LANES))
    copies = []
    for d in range(1, members):
        copy = pltpu.make_async_remote_copy(
            src_ref=sum_ref,
            dst_ref=sum_landed.at[d - 1],
            send_sem=fx_send.at[d - 1],
            recv_sem=fx_recv.at[d - 1],
            device_id=member(d),
            device_id_type=MESH,
        )
        copy.start()
        copies.append(copy)

    both = jnp.concatenate([flux_cells, curve_cells, jnp.zeros((6, LANES), F32)], axis=0)
    spread = pick_sum(jnp.concatenate([weights, unit, both], axis=0), cell_lane[...])
    blocks = width // LANES
    windows = jnp.concatenate(
        [shifted[0:ext_rows, LANES * h : LANES * h + 2 * LANES] for h in range(blocks)], axis=0
    )
    columns = dot3(split2(windows), (fcol[0], fcol[1]))
    for which in range(2):
        for h in range(blocks):
            for b in range(ORDERS):
                acc = None
                for a in range(ORDERS):
                    k = 32 * which + ORDERS * a + b
                    term = spread[k : k + 1, LANES * h : LANES * (h + 1)] * columns[
                        ext_rows * h : ext_rows * (h + 1), LANES * a : LANES * (a + 1)
                    ]
                    acc = term if acc is None else acc + term
                high, low = split2(acc)
                spot = (slice(ext_rows * b, ext_rows * (b + 1)), slice(width * which + LANES * h, width * which + LANES * (h + 1)))
                combined_h[spot] = high
                combined_l[spot] = low
    matched = dot3((frow[0], frow[1]), (combined_h[...], combined_l[...]))
    total = sum_ref[...]
    for d in range(1, members):
        copies[d - 1].wait_recv()
        total = total + sum_landed[d - 1]
    mean_flux = total[0:1, 0:1] * (1.0 / (cells * members))
    correction = (mean_flux - spread[64:65]) / spread[65:66]
    out_ref[...] = image_ref[...] - matched[:, 0:width] - correction * matched[:, width:]
    for copy in copies:
        copy.wait_send()


def fused(owner, offsets, slot, image, filters, counts):
    width = image.shape[2]
    cells = width // CELL
    visits = counts[1]
    members = counts[0] * counts[2]
    sums = filters.sum(axis=1)
    flux = (sums[:, None] * sums[None, :]).reshape(-1)
    consts = constants(filters, cells)
    pair_rows = sum(32 - 8 * (k // 8) for k in range(NBASIS))
    deep = ORDERS * (ROWS + 2 * PAD)
    full = width + 2 * LANES
    dma = pltpu.SemaphoreType.DMA
    hbm = pl.BlockSpec(memory_space=pltpu.HBM)
    return pl.pallas_call(
        lambda *refs: fused_kernel(counts, flux, *refs),
        name="difference_patch",
        out_shape=jax.ShapeDtypeStruct((ROWS, width), F32),
        in_specs=[hbm] * (4 + len(consts)),
        out_specs=pl.BlockSpec(memory_space=pltpu.VMEM),
        scratch_shapes=[
            pltpu.SMEM(owner.shape, jnp.int32),
            pltpu.SMEM(offsets.shape, jnp.int32),
            pltpu.VMEM((ROWS // visits, width), F32),
            pltpu.VMEM((ROWS, width), F32),
        ]
        + [pltpu.VMEM(const.shape, const.dtype) for const in consts]
        + [
            pltpu.VMEM((ROWS + 2 * PAD, full), F32),
            pltpu.VMEM((visits - 1, ROWS // visits, width), F32),
            pltpu.VMEM((ROWS + 2 * PAD + 8, full), F32),
            pltpu.VMEM((32, STAMP, cells * STAMP), F32),
            pltpu.VMEM((pair_rows, cells * STAMP), F32),
            pltpu.VMEM((deep, 2 * width), BF16),
            pltpu.VMEM((deep, 2 * width), BF16),
            pltpu.VMEM((8, LANES), F32),
            pltpu.VMEM((members - 1, 8, LANES), F32),
            dma((10,)),
            dma((visits - 1,)),
            dma((visits - 1,)),
            dma((visits - 1,)),
            dma((visits - 1,)),
            dma((8,)),
            dma((8,)),
            dma((members - 1,)),
            dma((members - 1,)),
        ],
        compiler_params=pltpu.CompilerParams(
            collective_id=0, has_side_effects=True, vmem_limit_bytes=48 << 20
        ),
    )(owner, offsets, slot, image, *consts)


def solution(mesh):
    counts = (mesh.shape["sky"], mesh.shape["visit"], mesh.shape["patch"])
    filters = filter_bank()

    def body(template_store, science, owner_visit, stamp_offset):
        return fused(owner_visit, stamp_offset, template_store, science, filters, counts)[None]

    spec = P("visit", "patch", "sky")
    in_specs = (spec, spec, P("sky", "patch"), P(None, "visit", "patch", "sky"))
    return jax.shard_map(body, mesh=mesh, in_specs=in_specs, out_specs=spec, check_vma=False)
```

time: 44.1 us -> 34.5 us (0.78)
  Pallas kernels: 31.5 us -> 25.2 us
  local copies, waits for them, and re-layouts: 9.93 us -> 8.18 us
  between operations: 1.46 us -> 0.69 us
  other arithmetic: 0.68 us -> 0 us
    pallas_call x3 -> x1, Pallas kernels: 31.5 us -> 25.2 us  [fused(): pl.pallas_call(lambda *refs: fused_kernel(counts, flux, *refs), name='dif...]
    slice x1 -> x0, local copies, waits for them, and re-layouts: 1.19 us -> none  [body(): mean_flux = total[0:1, 0:1] / stamps]
    broadcast_in_dim x1 -> x0, other arithmetic: 0.67 us -> none  [body(): return (resid - correction * unit)[None]]
    unnamed x28 -> x19, local copies, waits for them, and re-layouts: 8.74 us -> 8.18 us
where the time goes in v1:
time: 34.5 us; the launch traced here: 34.1 us
  Pallas kernels  25.2 us (73%)
  local copies, waits for them, and re-layouts  8.18 us (24%)
  between operations  0.69 us (2%)
    pallas_call x1, Pallas kernels, fused(): pl.pallas_call(lambda *refs: fused_kernel(counts, flux, *refs), name='dif...  25.2 us
    unnamed x19, local copies, waits for them, and re-layouts  8.18 us

profile of v1, /device:TPU:0, one launch (start us, length us, event | category | flops | bytes accessed | tf_op | source)
XLA Modules:
  0.0 34.1 jit_solution(11761087595684331484)
XLA Ops:
  0.0 0.0 copy-start.8
  0.7 0.0 copy-done.8
  0.7 0.0 copy-start
  0.7 1.1 %copy-done = bf16[2,256,640]{2,1,0:T(8,128)(2,1)S(1)} copy-done((bf16[2,256,640]{2,1,0:T(8,128)(2,1)S(1)}, bf16[2,256,640]{2,1,0:T(8,128)(2,1)}, u32[]{:S(2)}) %copy-start) | copy-done | bytes 655384
  1.8 0.0 copy-start.1
  1.8 1.1 %copy-done.1 = bf16[2,256,640]{2,1,0:T(8,128)(2,1)S(1)} copy-done((bf16[2,256,640]{2,1,0:T(8,128)(2,1)S(1)}, bf16[2,256,640]{2,1,0:T(8,128)(2,1)}, u32[]{:S(2)}) %copy-start.1) | copy-done | bytes 655384
  2.9 0.0 copy-start.2
  2.9 0.9 %copy-done.2 = f32[1,64,512]{2,1,0:T(8,128)S(1)} copy-done((f32[1,64,512]{2,1,0:T(8,128)S(1)}, f32[1,64,512]{2,1,0:T(8,128)}, u32[]{:S(2)}) %copy-start.2) | copy-done | bytes 131096
  3.8 0.0 copy-start.3
  3.8 0.9 %copy-done.3 = f32[1,64,512]{2,1,0:T(8,128)S(1)} copy-done((f32[1,64,512]{2,1,0:T(8,128)S(1)}, f32[1,64,512]{2,1,0:T(8,128)}, u32[]{:S(2)}) %copy-start.3) | copy-done | bytes 131096
  4.7 0.0 copy-start.4
  4.7 0.9 %copy-done.4 = bf16[128,512]{1,0:T(8,128)(2,1)S(1)} copy-done((bf16[128,512]{1,0:T(8,128)(2,1)S(1)}, bf16[128,512]{1,0:T(8,128)(2,1)}, u32[]{:S(2)}) %copy-start.4) | copy-done | bytes 131096
  5.6 0.0 copy-start.5
  5.6 0.9 %copy-done.5 = bf16[2,64,480]{2,1,0:T(8,128)(2,1)S(1)} copy-done((bf16[2,64,480]{2,1,0:T(8,128)(2,1)S(1)}, bf16[2,64,480]{2,1,0:T(8,128)(2,1)}, u32[]{:S(2)}) %copy-start.5) | copy-done | bytes 122904
  6.5 0.0 copy-start.6
  6.5 0.9 %copy-done.6 = bf16[2,160,64]{2,1,0:T(8,128)(2,1)S(1)} copy-done((bf16[2,160,64]{2,1,0:T(8,128)(2,1)S(1)}, bf16[2,160,64]{2,1,0:T(8,128)(2,1)}, u32[]{:S(2)}) %copy-start.6) | copy-done | bytes 40984
  7.4 0.0 copy-start.7
  7.4 0.8 %copy-done.7 = bf16[256,128]{1,0:T(8,128)(2,1)S(1)} copy-done((bf16[256,128]{1,0:T(8,128)(2,1)S(1)}, bf16[256,128]{1,0:T(8,128)(2,1)}, u32[]{:S(2)}) %copy-start.7) | copy-done | bytes 65560
  8.2 25.2 %difference_patch.1 = f32[64,512]{1,0:T(8,128)S(1)} custom-call(s32[1,1]{1,0:T(1,128)S(6)} %copy.12.refs_0_, s32[2,1,1,8]{3,2,1,0:T(1,128)S(1)} %copy-done.8, f32[1,64,512]{2,1,0:T(8,128)S(1)} %copy-done.2, f32[1,64,512]{2,1,0:T(8,128)S(1)} %copy-done.3, bf16[2,160,64]{2,1,0:T(8,128)(2,1)S(1)} %copy-done.6, bf16[2,256,640]{2,1,0:T(8,128)(2,1)S(1)} %copy-done.1, ...), custom_call_target="tpu_custom_call" | custom-call | tf_op jit(solution)/shard_map/difference_patch/pallas_call | solution.py:388
  33.4 0.7 %copy.13 = f32[1,64,512]{2,1,0:T(8,128)} copy(f32[1,64,512]{2,1,0:T(8,128)S(1)} %bitcast.1) | data formatting | bytes 262144
Async XLA Ops:
  0.0 0.7 %copy-start.8 = (s32[2,1,1,8]{3,2,1,0:T(1,128)S(1)}, s32[2,1,1,8]{3,2,1,0:T(1,128)}, u32[]{:S(2)}) copy-start(s32[2,1,1,8]{3,2,1,0:T(1,128)} %refs_1_.1) | copy-start | bytes 196
  0.7 1.1 %copy-start = (bf16[2,256,640]{2,1,0:T(8,128)(2,1)S(1)}, bf16[2,256,640]{2,1,0:T(8,128)(2,1)}, u32[]{:S(2)}) copy-start(bf16[2,256,640]{2,1,0:T(8,128)(2,1)} %constant.14.clone.refs_6_) | copy-start | bytes 1966084
  1.8 1.1 %copy-start.1 = (bf16[2,256,640]{2,1,0:T(8,128)(2,1)S(1)}, bf16[2,256,640]{2,1,0:T(8,128)(2,1)}, u32[]{:S(2)}) copy-start(bf16[2,256,640]{2,1,0:T(8,128)(2,1)} %constant.13.clone.refs_5_) | copy-start | bytes 1966084
  2.9 0.9 %copy-start.2 = (f32[1,64,512]{2,1,0:T(8,128)S(1)}, f32[1,64,512]{2,1,0:T(8,128)}, u32[]{:S(2)}) copy-start(f32[1,64,512]{2,1,0:T(8,128)} %refs_2_.1) | copy-start | bytes 393220
  3.8 0.9 %copy-start.3 = (f32[1,64,512]{2,1,0:T(8,128)S(1)}, f32[1,64,512]{2,1,0:T(8,128)}, u32[]{:S(2)}) copy-start(f32[1,64,512]{2,1,0:T(8,128)} %refs_3_.1) | copy-start | bytes 393220
  4.7 0.9 %copy-start.4 = (bf16[128,512]{1,0:T(8,128)(2,1)S(1)}, bf16[128,512]{1,0:T(8,128)(2,1)}, u32[]{:S(2)}) copy-start(bf16[128,512]{1,0:T(8,128)(2,1)} %constant.17.clone.refs_9_) | copy-start | bytes 393220
  5.6 0.9 %copy-start.5 = (bf16[2,64,480]{2,1,0:T(8,128)(2,1)S(1)}, bf16[2,64,480]{2,1,0:T(8,128)(2,1)}, u32[]{:S(2)}) copy-start(bf16[2,64,480]{2,1,0:T(8,128)(2,1)} %constant.15.clone.refs_7_) | copy-start | bytes 368644
  6.5 0.9 %copy-start.6 = (bf16[2,160,64]{2,1,0:T(8,128)(2,1)S(1)}, bf16[2,160,64]{2,1,0:T(8,128)(2,1)}, u32[]{:S(2)}) copy-start(bf16[2,160,64]{2,1,0:T(8,128)(2,1)} %constant.12.clone.refs_4_) | copy-start | bytes 122884
  7.4 0.8 %copy-start.7 = (bf16[256,128]{1,0:T(8,128)(2,1)S(1)}, bf16[256,128]{1,0:T(8,128)(2,1)}, u32[]{:S(2)}) copy-start(bf16[256,128]{1,0:T(8,128)(2,1)} %constant.16.clone.refs_8_) | copy-start | bytes 196612

commit v2 on v1

--- a/solution.py
+++ b/solution.py
@@ -419,7 +419,7 @@
             dma((members - 1,)),
         ],
         compiler_params=pltpu.CompilerParams(
-            collective_id=0, has_side_effects=True, vmem_limit_bytes=48 << 20
+            collective_id=0, has_side_effects=True, vmem_limit_bytes=56 << 20
         ),
     )(owner, offsets, slot, image, *consts)
 

time: 34.5 us -> 28.5 us (0.83)
  local copies, waits for them, and re-layouts: 8.18 us -> 1.57 us
  Pallas kernels: 25.2 us -> 26.1 us
    unnamed x19 -> x1, local copies, waits for them, and re-layouts: 8.18 us -> 1.57 us
    pallas_call x1, Pallas kernels: 25.2 us -> 26.1 us  [fused(): pl.pallas_call(lambda *refs: fused_kernel(counts, flux, *refs), name='dif...]
where the time goes in v2:
time: 28.5 us; the launch traced here: 28.3 us
  Pallas kernels  26.1 us (92%)
  local copies, waits for them, and re-layouts  1.57 us (6%)
  between operations  0.66 us (2%)
    pallas_call x1, Pallas kernels, fused(): pl.pallas_call(lambda *refs: fused_kernel(counts, flux, *refs), name='dif...  26.1 us
    unnamed x1, local copies, waits for them, and re-layouts  1.57 us

profile of v2, /device:TPU:0, one launch (start us, length us, event | category | flops | bytes accessed | tf_op | source)
XLA Modules:
  0.0 28.3 jit_solution(7148893134360983546)
XLA Ops:
  0.7 26.1 %difference_patch.1 = f32[64,512]{1,0:T(8,128)} custom-call(s32[1,1]{1,0:T(1,128)S(6)} %copy.12.refs_0_, s32[2,1,1,8]{3,2,1,0:T(1,128)} %refs_1_.1, f32[1,64,512]{2,1,0:T(8,128)} %refs_2_.1, f32[1,64,512]{2,1,0:T(8,128)} %refs_3_.1, bf16[2,160,64]{2,1,0:T(8,128)(2,1)} %constant.12.clone.refs_4_, bf16[2,256,640]{2,1,0:T(8,128)(2,1)} %constant.13.clone.refs_5_, ...), custom_call_target="tpu_custom_call" | custom-call | tf_op jit(solution)/shard_map/difference_patch/pallas_call | solution.py:388
  26.8 1.6 %copy.13 = f32[1,64,512]{2,1,0:T(8,128)} copy(f32[1,64,512]{2,1,0:T(8,128)} %bitcast.1) | data formatting | bytes 262144

commit v3 on v2

--- a/solution.py
+++ b/solution.py
@@ -124,7 +124,7 @@
     srow_hbm, scol_hbm, fcol_hbm, frow_hbm, pick_hbm, put_hbm,
     out_ref,
     owner_ref, offset_ref, mine_ref, image_ref, srow, scol, fcol, frow, lane_cell, cell_lane,
-    ext, landed, shifted, stamps, pairs, combined_h, combined_l, sum_ref, sum_landed,
+    ext, landed, edge, edge_landed, shifted, stamps, pairs, combined_h, combined_l, sum_ref, sum_landed,
     local_sem, rs_send, rs_recv, ag_send, ag_recv, ha_send, ha_recv, fx_send, fx_recv,
 ):
     sky_count, visits, patches = counts
@@ -241,15 +241,26 @@
             device_id_type=MESH,
         ).wait_recv()
 
-    row_span = {-1: (PAD, PAD + ROWS, PAD), 0: (PAD, PAD, ROWS), 1: (ROWS, 0, PAD)}
-    col_span = {-1: (LANES, LANES + width, LANES), 0: (LANES, LANES, width), 1: (width, 0, LANES)}
+    lane8 = lax.broadcasted_iota(jnp.int32, (8, LANES), 1) // PAD
+    for side, (first, base) in enumerate(((LANES, 0), (width, LANES - PAD))):
+        merged = jnp.zeros((8, LANES), F32)
+        for r in range(ROWS // 8):
+            block = ext[PAD + 8 * r : PAD + 8 * r + 8, first : first + LANES]
+            merged = jnp.where(lane8 == r, pltpu.roll(block, (PAD * r - base) % LANES, 1), merged)
+        edge[side] = merged
+    row_span = {-1: (PAD, PAD + ROWS), 1: (ROWS, 0)}
     edges = []
     for way, (ds, dp) in enumerate(ways):
-        row_src, row_dst, row_len = row_span[dp]
-        col_src, col_dst, col_len = col_span[ds]
+        if ds == 0:
+            row_src, row_dst = row_span[dp]
+            source = ext.at[pl.ds(row_src, PAD), pl.ds(LANES, width)]
+            target = ext.at[pl.ds(row_dst, PAD), pl.ds(LANES, width)]
+        else:
+            source = edge.at[(ds + 1) // 2]
+            target = edge_landed.at[way]
         copy = pltpu.make_async_remote_copy(
-            src_ref=ext.at[pl.ds(row_src, row_len), pl.ds(col_src, col_len)],
-            dst_ref=ext.at[pl.ds(row_dst, row_len), pl.ds(col_dst, col_len)],
+            src_ref=source,
+            dst_ref=target,
             send_sem=ha_send.at[way],
             recv_sem=ha_recv.at[way],
             device_id=there(ds, dp),
@@ -267,13 +278,21 @@
         copy.wait_send()
     for way, (ds, dp) in enumerate(ways):
 
+        @pl.when(exists(-ds, -dp))
+        def _():
+            edges[way].wait_recv()
+            if ds != 0:
+                first, base = (full - LANES, 0) if ds < 0 else (0, LANES - PAD)
+                spans = {0: (0, ROWS // 8, PAD), -1: (0, 2, PAD + ROWS), 1: (ROWS // 8 - 2, 2, 0)}
+                group, number, row = spans[dp]
+                packed = edge_landed[way]
+                for r in range(number):
+                    moved = pltpu.roll(packed, (base - PAD * (group + r)) % LANES, 1)
+                    ext[row + 8 * r : row + 8 * r + 8, first : first + LANES] = moved
+
         @pl.when(exists(ds, dp))
         def _():
             edges[way].wait_send()
-
-        @pl.when(exists(-ds, -dp))
-        def _():
-            edges[way].wait_recv()
 
     shifted[0:ext_rows, :] = pltpu.roll(ext[...], full - (LANES - PAD), 1)
     shifted[ext_rows:, :] = jnp.zeros((8, full), F32)
@@ -401,6 +420,8 @@
         + [
             pltpu.VMEM((ROWS + 2 * PAD, full), F32),
             pltpu.VMEM((visits - 1, ROWS // visits, width), F32),
+            pltpu.VMEM((2, 8, LANES), F32),
+            pltpu.VMEM((8, 8, LANES), F32),
             pltpu.VMEM((ROWS + 2 * PAD + 8, full), F32),
             pltpu.VMEM((32, STAMP, cells * STAMP), F32),
             pltpu.VMEM((pair_rows, cells * STAMP), F32),

time: 28.5 us -> 28.1 us (0.986)
  Pallas kernels: 26.1 us -> 25.8 us
    pallas_call x1, Pallas kernels: 26.1 us -> 25.8 us  [fused(): pl.pallas_call(lambda *refs: fused_kernel(counts, flux, *refs), name='dif...]
where the time goes in v3:
time: 28.1 us; the launch traced here: 28 us
  Pallas kernels  25.8 us (92%)
  local copies, waits for them, and re-layouts  1.57 us (6%)
  between operations  0.66 us (2%)
    pallas_call x1, Pallas kernels, fused(): pl.pallas_call(lambda *refs: fused_kernel(counts, flux, *refs), name='dif...  25.8 us
    unnamed x1, local copies, waits for them, and re-layouts  1.57 us

profile of v3, /device:TPU:0, one launch (start us, length us, event | category | flops | bytes accessed | tf_op | source)
XLA Modules:
  0.0 28.0 jit_solution(14942537044827695251)
XLA Ops:
  0.7 25.8 %difference_patch.1 = f32[64,512]{1,0:T(8,128)} custom-call(s32[1,1]{1,0:T(1,128)S(6)} %copy.12.refs_0_, s32[2,1,1,8]{3,2,1,0:T(1,128)} %refs_1_.1, f32[1,64,512]{2,1,0:T(8,128)} %refs_2_.1, f32[1,64,512]{2,1,0:T(8,128)} %refs_3_.1, bf16[2,160,64]{2,1,0:T(8,128)(2,1)} %constant.12.clone.refs_4_, bf16[2,256,640]{2,1,0:T(8,128)(2,1)} %constant.13.clone.refs_5_, ...), custom_call_target="tpu_custom_call" | custom-call | tf_op jit(solution)/shard_map/difference_patch/pallas_call | solution.py:407
  26.4 1.6 %copy.13 = f32[1,64,512]{2,1,0:T(8,128)} copy(f32[1,64,512]{2,1,0:T(8,128)} %bitcast.1) | data formatting | bytes 262144

commit v4 on v3

--- a/solution.py
+++ b/solution.py
@@ -440,9 +440,9 @@
             dma((members - 1,)),
         ],
         compiler_params=pltpu.CompilerParams(
-            collective_id=0, has_side_effects=True, vmem_limit_bytes=56 << 20
+            collective_id=0, has_side_effects=True, vmem_limit_bytes=40 << 20
         ),
-    )(owner, offsets, slot, image, *consts)
+    )(owner, *[pltpu.with_memory_space_constraint(v, pltpu.HBM) for v in (offsets, slot, image, *consts)])
 
 
 def solution(mesh):

time: 28.1 us -> 26.6 us (0.947)
  local copies, waits for them, and re-layouts: 1.57 us -> 0.66 us
  Pallas kernels: 25.8 us -> 25.1 us
    unnamed x1, local copies, waits for them, and re-layouts: 1.57 us -> 0.66 us
    pallas_call x1, Pallas kernels: 25.8 us -> 25.1 us  [fused(): pl.pallas_call(lambda *refs: fused_kernel(counts, flux, *refs), name='dif...]
where the time goes in v4:
time: 26.6 us; the launch traced here: 26.4 us
  Pallas kernels  25.1 us (94%)
  local copies, waits for them, and re-layouts  0.66 us (2%)
  between operations  0.66 us (2%)
    pallas_call x1, Pallas kernels, fused(): pl.pallas_call(lambda *refs: fused_kernel(counts, flux, *refs), name='dif...  25.1 us
    unnamed x1, local copies, waits for them, and re-layouts  0.66 us

profile of v4, /device:TPU:0, one launch (start us, length us, event | category | flops | bytes accessed | tf_op | source)
XLA Modules:
  0.0 26.4 jit_solution(11137689510125127926)
XLA Ops:
  0.7 25.1 %difference_patch.1 = f32[64,512]{1,0:T(8,128)S(1)} custom-call(s32[1,1]{1,0:T(1,128)S(6)} %copy.12.refs_0_, s32[2,1,1,8]{3,2,1,0:T(1,128)} %refs_1_.1, f32[1,64,512]{2,1,0:T(8,128)} %refs_2_.1, f32[1,64,512]{2,1,0:T(8,128)} %refs_3_.1, bf16[2,160,64]{2,1,0:T(8,128)(2,1)} %constant.12.clone.refs_4_, bf16[2,256,640]{2,1,0:T(8,128)(2,1)} %constant.13.clone.refs_5_, ...), custom_call_target="tpu_custom_call" | custom-call | tf_op jit(solution)/shard_map/difference_patch/pallas_call | solution.py:407
  25.8 0.7 %copy.13 = f32[1,64,512]{2,1,0:T(8,128)} copy(f32[1,64,512]{2,1,0:T(8,128)S(1)} %bitcast.1) | data formatting | bytes 262144

commit v5 on v4

--- a/solution.py
+++ b/solution.py
@@ -123,7 +123,7 @@
     counts, flux, owner_hbm, offset_hbm, slot_hbm, image_hbm,
     srow_hbm, scol_hbm, fcol_hbm, frow_hbm, pick_hbm, put_hbm,
     out_ref,
-    owner_ref, offset_ref, mine_ref, image_ref, srow, scol, fcol, frow, lane_cell, cell_lane,
+    owner_ref, offset_ref, slot_ref, image_ref, srow, scol, fcol, frow, lane_cell, cell_lane,
     ext, landed, edge, edge_landed, shifted, stamps, pairs, combined_h, combined_l, sum_ref, sum_landed,
     local_sem, rs_send, rs_recv, ag_send, ag_recv, ha_send, ha_recv, fx_send, fx_recv,
 ):
@@ -152,9 +152,9 @@
 
     own_rows = pl.ds(pl.multiple_of(visit * chunk, chunk), chunk)
     moves = [
+        (slot_hbm.at[0], slot_ref),
         (owner_hbm, owner_ref),
         (offset_hbm, offset_ref),
-        (slot_hbm.at[0, own_rows, :], mine_ref),
         (image_hbm.at[0], image_ref),
         (srow_hbm, srow),
         (scol_hbm, scol),
@@ -170,20 +170,21 @@
     ext[PAD : PAD + ROWS, 0:LANES] = jnp.zeros((ROWS, LANES), F32)
     ext[PAD : PAD + ROWS, full - LANES :] = jnp.zeros((ROWS, LANES), F32)
 
+    for load in loads:
+        load.start()
     barrier = pltpu.get_barrier_semaphore()
     for d in range(1, visits):
         pl.semaphore_signal(barrier, inc=1, device_id={"visit": lax.rem(visit + d, visits)}, device_id_type=MESH)
     for d in range(1, members):
         pl.semaphore_signal(barrier, inc=1, device_id=member(d), device_id_type=MESH)
-    for load in loads:
-        load.start()
     pl.semaphore_wait(barrier, visits - 1 + members - 1)
 
+    loads[0].wait()
     scatter = []
     for d in range(1, visits):
         to = lax.rem(visit + d, visits)
         copy = pltpu.make_async_remote_copy(
-            src_ref=slot_hbm.at[0, pl.ds(pl.multiple_of(to * chunk, chunk), chunk), :],
+            src_ref=slot_ref.at[pl.ds(pl.multiple_of(to * chunk, chunk), chunk), :],
             dst_ref=landed.at[d - 1],
             send_sem=rs_send.at[d - 1],
             recv_sem=rs_recv.at[d - 1],
@@ -192,7 +193,7 @@
         )
         copy.start()
         scatter.append(copy)
-    for load in loads:
+    for load in loads[1:]:
         load.wait()
     groups = cells // 4
     lane = lax.broadcasted_iota(jnp.int32, (STAMP, LANES), 1)
@@ -210,7 +211,7 @@
         stamps[spare] = jnp.zeros((STAMP, cells * STAMP), F32)
 
     owner = owner_ref[0, 0]
-    current = jnp.where(owner == visit, mine_ref[...], 0.0)
+    current = jnp.where(owner == visit, slot_ref[own_rows, :], 0.0)
     for d in range(1, visits):
         scatter[d - 1].wait_recv()
         source = lax.rem(visit + visits - d, visits)
@@ -413,7 +414,7 @@
         scratch_shapes=[
             pltpu.SMEM(owner.shape, jnp.int32),
             pltpu.SMEM(offsets.shape, jnp.int32),
-            pltpu.VMEM((ROWS // visits, width), F32),
+            pltpu.VMEM((ROWS, width), F32),
             pltpu.VMEM((ROWS, width), F32),
         ]
         + [pltpu.VMEM(const.shape, const.dtype) for const in consts]

time: 26.6 us -> 26.4 us (level)
  no operation moved by 1% of the time
where the time goes in v5:
time: 26.4 us; the launch traced here: 26.2 us
  Pallas kernels  24.9 us (94%)
  local copies, waits for them, and re-layouts  0.66 us (2%)
  between operations  0.66 us (2%)
    pallas_call x1, Pallas kernels, fused(): pl.pallas_call(lambda *refs: fused_kernel(counts, flux, *refs), name='dif...  24.9 us
    unnamed x1, local copies, waits for them, and re-layouts  0.66 us

profile of v5, /device:TPU:0, one launch (start us, length us, event | category | flops | bytes accessed | tf_op | source)
XLA Modules:
  0.0 26.2 jit_solution(684864849878504562)
XLA Ops:
  0.7 24.9 %difference_patch.1 = f32[64,512]{1,0:T(8,128)S(1)} custom-call(s32[1,1]{1,0:T(1,128)S(6)} %copy.12.refs_0_, s32[2,1,1,8]{3,2,1,0:T(1,128)} %refs_1_.1, f32[1,64,512]{2,1,0:T(8,128)} %refs_2_.1, f32[1,64,512]{2,1,0:T(8,128)} %refs_3_.1, bf16[2,160,64]{2,1,0:T(8,128)(2,1)} %constant.12.clone.refs_4_, bf16[2,256,640]{2,1,0:T(8,128)(2,1)} %constant.13.clone.refs_5_, ...), custom_call_target="tpu_custom_call" | custom-call | tf_op jit(solution)/shard_map/difference_patch/pallas_call | solution.py:408
  25.6 0.7 %copy.13 = f32[1,64,512]{2,1,0:T(8,128)} copy(f32[1,64,512]{2,1,0:T(8,128)S(1)} %bitcast.1) | data formatting | bytes 262144
